TPU v7x, 256 devices: a whole 4x4x8 slice. The times are simulated.
256 devices in a mesh: dom: 32 (over x, z), grp: 8 (over y, core).
Axes of the slice: x: 4, y: 4, z: 8, core: 2. Of those that a mesh axis runs over, the one named last changes fastest.
Arguments:
- node_feats: bfloat16 [65536, 1024], P(('dom', 'grp')), may hold values from -6 to 6
- weight: bfloat16 [1024, 512], replicated, may hold values from -0.1875 to 0.1875
- bias: float32 [512], replicated, may hold values from -4 to 4
- cotangent: bfloat16 [65536, 512], P(('dom', 'grp')), may hold values from -6 to 6
- tile_bank: bfloat16 [16, 128, 128], replicated, may hold values from -0.125 to 0.125
- local_cols: int32 [32, 16, 16], P('dom'), may hold values from 0 to 15
- local_banks: int32 [32, 16, 16], P('dom'), may hold values from 0 to 15
- published: int32 [32, 4], P('dom'), may hold values from 0 to 15, as said below
- send_table: int32 [32, 32, 2], replicated, may hold values from -1 to 3, as said below
- halo_rows: int32 [32, 32, 2], P('dom'), may hold values from 0 to 15
- halo_banks: int32 [32, 32, 2], P('dom'), may hold values from 0 to 15
Outputs:
- activations: bfloat16 [65536, 512], P(('dom', 'grp'))
- grad_nodes: bfloat16 [65536, 1024], P(('dom', 'grp'))
- grad_weight: float32 [1024, 512], replicated
- grad_bias: float32 [512], replicated
Inputs may be any that keep to these rules, and one draw needn't show every extreme that they name: `published`: the 4 entries of a partition are distinct block numbers of that partition; 0 and 15 each appear in some partition's list. `send_table`: entry s of the pair (src, p) is -1 or an index into the offered list of src; the live entries of a pair come first and are distinct; a pair (p, p) has none; some pair has all 2 entries live.
All inputs are finite; a program needn't handle non-finite values.
Results may differ from a plain program's by a relative error of at most 0.019.
The roundings to bfloat16 on the way count: a program that leaves them out, or rounds other values in their place, can miss the bound.
Values may be sent and summed in bfloat16 or wider, within the bound.
A program may use at most 64 MiB of HBM per device.

v0:
```python
import jax
import jax.numpy as jnp
from jax import lax
from jax.sharding import PartitionSpec as P


def per_device(
    node_feats,
    weight,
    bias,
    cotangent,
    tile_bank,
    local_cols,
    local_banks,
    published,
    send_table,
    halo_rows,
    halo_banks,
):
    domains = lax.axis_size("dom")
    groups = lax.axis_size("grp")
    domain_index = lax.axis_index("dom")
    rows_here = node_feats.shape[0]
    tile_size = tile_bank.shape[1]
    slot_count = send_table.shape[2]
    pub_count = published.shape[1]
    tiles_row = local_cols.shape[2]
    features = lax.all_to_all(node_feats, "grp", split_axis=1, concat_axis=0, tiled=True)
    part_rows, narrow = features.shape
    blocks = part_rows // tile_size
    feat_blocks = features.reshape(blocks, tile_size, narrow)
    cols_here = local_cols[0]
    banks_here = local_banks[0]
    own_pub = published[0]
    incoming = lax.dynamic_index_in_dim(send_table, domain_index, 1, keepdims=False)
    live_in = (incoming >= 0).astype(jnp.float32)[:, :, None, None]
    rows_in = halo_rows[0]
    halo_tiles = tile_bank[halo_banks[0]]
    source_ids = lax.broadcasted_iota(jnp.int32, (domains, slot_count), 0)
    gathered_ids = source_ids * pub_count + jnp.maximum(incoming, 0)

    def forward_tiles(position, running):
        column = lax.dynamic_index_in_dim(cols_here, position, 1, keepdims=False)
        bank_ids = lax.dynamic_index_in_dim(banks_here, position, 1, keepdims=False)
        return running + jnp.einsum(
            "rij,rjf->rif",
            tile_bank[bank_ids],
            feat_blocks[column],
            preferred_element_type=jnp.float32,
        )

    running = lax.fori_loop(
        0, tiles_row, forward_tiles, jnp.zeros((blocks, tile_size, narrow), jnp.float32)
    )
    shared = feat_blocks[own_pub]
    everyone = lax.all_gather(shared, "dom", axis=0, tiled=True)
    remote = everyone[gathered_ids]
    halo_terms = (
        jnp.einsum("dsij,dsjf->dsif", halo_tiles, remote, preferred_element_type=jnp.float32)
        * live_in
    )
    running = running + jax.ops.segment_sum(
        halo_terms.reshape(domains * slot_count, tile_size, narrow),
        rows_in.reshape(-1),
        num_segments=blocks,
    )
    agg_narrow = running.astype(jnp.bfloat16).reshape(part_rows, narrow)
    aggregated = lax.all_to_all(agg_narrow, "grp", split_axis=0, concat_axis=1, tiled=True)
    pre_act = jnp.dot(aggregated, weight, preferred_element_type=jnp.float32) + bias
    activations = jnp.maximum(pre_act, 0.0).astype(jnp.bfloat16)
    grad_pre = jnp.where(pre_act > 0, cotangent.astype(jnp.float32), 0.0).astype(jnp.bfloat16)
    weight_part = lax.dot_general(
        aggregated, grad_pre, (((0,), (0,)), ((), ())), preferred_element_type=jnp.float32
    )
    bias_part = jnp.sum(grad_pre.astype(jnp.float32), axis=0)
    grad_agg = lax.dot_general(
        grad_pre, weight, (((1,), (1,)), ((), ())), preferred_element_type=jnp.float32
    ).astype(jnp.bfloat16)
    grad_narrow = lax.all_to_all(grad_agg, "grp", split_axis=1, concat_axis=0, tiled=True)
    grad_blocks = grad_narrow.reshape(blocks, tile_size, narrow)

    def backward_tiles(position, running):
        column = lax.dynamic_index_in_dim(cols_here, position, 1, keepdims=False)
        bank_ids = lax.dynamic_index_in_dim(banks_here, position, 1, keepdims=False)
        contrib = jnp.einsum(
            "rji,rjf->rif", tile_bank[bank_ids], grad_blocks, preferred_element_type=jnp.float32
        )
        return running + jax.ops.segment_sum(contrib, column, num_segments=blocks)

    grad_total = lax.fori_loop(
        0, tiles_row, backward_tiles, jnp.zeros((blocks, tile_size, narrow), jnp.float32)
    )
    back_terms = (
        jnp.einsum(
            "dsji,dsjf->dsif", halo_tiles, grad_blocks[rows_in], preferred_element_type=jnp.float32
        )
        * live_in
    )
    placed = jax.ops.segment_sum(
        back_terms.reshape(domains * slot_count, tile_size, narrow),
        gathered_ids.reshape(-1),
        num_segments=domains * pub_count,
    )
    mine_back = lax.psum_scatter(placed, "dom", scatter_dimension=0, tiled=True)
    back_total = jax.ops.segment_sum(mine_back, own_pub, num_segments=blocks)
    grad_total = grad_total + back_total
    grad_nodes = lax.all_to_all(
        grad_total.astype(jnp.bfloat16).reshape(part_rows, narrow),
        "grp",
        split_axis=0,
        concat_axis=1,
        tiled=True,
    )
    norm_scale = float(rows_here * groups * domains) ** (-0.5)
    weight_total, bias_total = lax.psum((weight_part, bias_part), ("dom", "grp"))
    return (activations, grad_nodes, weight_total * norm_scale, bias_total * norm_scale)


def solution(mesh):
    in_specs = (
        P(("dom", "grp"), None),
        P(),
        P(),
        P(("dom", "grp"), None),
        P(),
        P("dom", None, None),
        P("dom", None, None),
        P("dom", None),
        P(),
        P("dom", None, None),
        P("dom", None, None),
    )
    out_specs = (P(("dom", "grp"), None), P(("dom", "grp"), None), P(), P())
    return jax.shard_map(
        per_device, mesh=mesh, in_specs=in_specs, out_specs=out_specs, check_vma=False
    )
```

profile of v0, /device:TPU:2, one launch (start us, length us, event | category | flops | bytes accessed | tf_op | source)
XLA Modules:
  0.0 686.9 jit_solution(15913844381797116386)
XLA Ops:
  9.3 4.5 all-to-all-start
  17.1 7.1 %all-to-all-done = bf16[256,8,128]{2,0,1:T(8,128)(2,1)} async-done(((bf16[256,8,128]{2,0,1:T(8,128)(2,1)}), bf16[256,8,128]{2,0,1:T(8,128)(2,1)}, u32[]{:S(2)}, u32[]{:S(2)}) %all-to-all-start) | async-done | bytes 524320 | tf_op jit(solution)/shard_map/all_to_all | solution.py:28
  26.5 74.0 %while.28 = (s32[]{:T(128)}, f32[16,128,128]{2,1,0:T(8,128)S(1)}, s32[16,16]{0,1:T(8,128)S(1)}, bf16[16,128,128]{2,1,0:T(8,128)(2,1)S(1)}, s32[16,16]{0,1:T(8,12...) while((s32[]{:T(128)}, f32[16,128,128]{2,1,0:T(8,128)S(1)}, ...), condition=%wide.region_1.2_spmd.clone, body=%wide.region_0.1_spmd.clone.sunk | while | flops 67635296 | bytes 5251683 | solution.py:52
  100.5 7.6 %all-gather.3.cloned.1.call-done = bf16[128,128,128]{2,1,0:T(8,128)(2,1)} async-done(((bf16[4,128,128]{2,1,0:T(8,128)(2,1)}), bf16[128,128,128]{2,1,0:T(8,128)(2,1)}) %all-gather.3.cloned.1.call-update) | async-done | bytes 4194320 | tf_op jit(solution)/shard_map/all_gather | solution.py:56
  108.1 4.3 gather_fusion.5
  112.4 4.9 convolution_multiply_fusion.1
  117.2 8.8 %scatter_fusion.1 = f32[16,128,128]{2,1,0:T(8,128)S(1)} fusion(f32[16,128,128]{2,1,0:T(8,128)S(1)} %get-tuple-element.222, s32[64]{0:T(128)S(1)} %reshape.272, f32[64,128,128]{2,1,0:T(8,128)} %bitcast.94), kind=kCustom, calls=%fused_computation.8 | custom fusion | flops 1048576 | bytes 12583168 | tf_op jit(solution)/shard_map/scatter-add | solution.py:62
  126.9 4.4 all-to-all-start.1
  131.6 10.1 %all-to-all-done.1 = bf16[8,256,128]{2,1,0:T(8,128)(2,1)S(1)} async-done(((bf16[8,256,128]{2,1,0:T(8,128)(2,1)}), bf16[8,256,128]{2,1,0:T(8,128)(2,1)S(1)}, u32[]{:S(2)}, u32[]{:S(2)}) %all-to-all-start.1) | async-done | bytes 524320 | tf_op jit(solution)/shard_map/all_to_all | solution.py:68
  144.6 3.5 all-to-all-start.2
  148.6 9.8 %all-to-all-done.2 = bf16[256,8,128]{2,0,1:T(8,128)(2,1)S(1)} async-done(((bf16[256,8,128]{2,0,1:T(8,128)(2,1)}), bf16[256,8,128]{2,0,1:T(8,128)(2,1)S(1)}, u32[]{:S(2)}, u32[]{:S(2)}) %all-to-all-start.2) | async-done | bytes 524320 | tf_op jit(solution)/shard_map/all_to_all | solution.py:79
  160.5 5.2 convolution_multiply_fusion
  165.8 4.3 broadcast_in_dim.12
  170.0 13.4 %scatter_fusion.2 = f32[128,128,128]{2,1,0:T(8,128)} fusion(f32[128,128,128]{2,1,0:T(8,128)} %broadcast_in_dim.12, s32[64]{0:T(128)S(1)} %add_bitcast_fusion, f32[64,128,128]{2,1,0:T(8,128)} %bitcast.93), kind=kCustom, calls=%fused_computation.9 | custom fusion | flops 1048576 | bytes 12583168 | tf_op jit(solution)/shard_map/scatter-add | solution.py:99
  183.5 75.8 %psum.15 = f32[512]{0:T(512)S(1)} all-reduce(f32[512]{0:T(512)S(1)} %get-tuple-element.277), channel_id=1, replica_groups=mesh['dom'=32,'grp'=8] {'dom','grp'}, use_global_device_ids=true, to_apply=%region_11.12 | all-reduce | flops 512 | bytes 4096 | tf_op jit(solution)/shard_map/psum | solution.py:115
  262.2 98.2 %while.27 = (s32[]{:T(128)}, f32[16,128,128]{2,1,0:T(8,128)}, s32[16,16]{0,1:T(8,128)S(1)}, s32[16,16]{0,1:T(8,128)S(1)}, bf16[16,128,128]{2,1,0:T(8,128)(2,1)S(...) while((s32[]{:T(128)}, f32[16,128,128]{2,1,0:T(8,128)}, s32[16,16]{0,1:T(8,128)S(1)}, ...), condition=%wide.region_5.6_spmd, body=%wide.region_3.5_spmd.sunk | while | flops 67372080 | bytes 6296081 | solution.py:90
  265.0 3.3 scatter_fusion
  283.4 3.3 scatter_fusion
  289.6 3.3 scatter_fusion
  301.9 3.3 scatter_fusion
  320.3 3.4 scatter_fusion
  360.4 48.2 %reduce-scatter.2.cloned.1.call-done = f32[4,128,128]{2,1,0:T(8,128)} async-done(((f32[128,128,128]{2,1,0:T(8,128)}), f32[4,128,128]{2,1,0:T(8,128)}) %reduce-scatter.2.cloned.1.call-update) | async-done | bytes 262160 | tf_op jit(solution)/shard_map/reduce_scatter | solution.py:104
  413.3 4.3 all-to-all-start.3
  418.1 257.9 %all-reduce.2.cloned.1.call-done = f32[1024,512]{1,0:T(8,128)} async-done(((f32[1024,512]{1,0:T(8,128)}), f32[1024,512]{1,0:T(8,128)}) %all-reduce.2.cloned.1.call-update) | async-done | bytes 2097168 | tf_op jit(solution)/shard_map/psum | solution.py:115
  (246 shorter events, 181.0 us)
Async XLA Ops:
  7.2 134.8 %copy-start = (bf16[1024,512]{1,0:T(8,128)(2,1)S(1)}, bf16[1024,512]{1,0:T(8,128)(2,1)}, u32[]{:S(2)}) copy-start(bf16[1024,512]{1,0:T(8,128)(2,1)} %param.16) | copy-start | bytes 3145732
  7.2 6.6 copy-start.3
  7.2 6.8 copy-start.8
  7.2 7.4 %copy-start.4 = (s32[1,16,16]{2,1,0:T(8,128)S(1)}, s32[1,16,16]{2,1,0:T(8,128)}, u32[]{:S(2)}) copy-start(s32[1,16,16]{2,1,0:T(8,128)} %param.21) | copy-start | bytes 3076
  7.2 7.4 %copy-start.5 = (s32[1,16,16]{2,1,0:T(8,128)S(1)}, s32[1,16,16]{2,1,0:T(8,128)}, u32[]{:S(2)}) copy-start(s32[1,16,16]{2,1,0:T(8,128)} %param.20) | copy-start | bytes 3076
  7.2 7.5 %copy-start.6 = (s32[1,32,2]{1,2,0:T(2,128)S(1)}, s32[1,32,2]{1,2,0:T(2,128)}, u32[]{:S(2)}) copy-start(s32[1,32,2]{1,2,0:T(2,128)} %param.24) | copy-start | bytes 772
  7.2 7.7 %copy-start.1 = (bf16[16,128,128]{2,1,0:T(8,128)(2,1)S(1)}, bf16[16,128,128]{2,1,0:T(8,128)(2,1)}, u32[]{:S(2)}) copy-start(bf16[16,128,128]{2,1,0:T(8,128)(2,1)} %param.19) | copy-start | bytes 1572868
  9.3 14.9 %all-to-all-start = ((bf16[256,8,128]{2,0,1:T(8,128)(2,1)}), bf16[256,8,128]{2,0,1:T(8,128)(2,1)}, u32[]{:S(2)}, u32[]{:S(2)}) async-start(bf16[256,8,128]{2,0,1:T(8,128)(2,1)} %copy_bitcast_fusion.1), calls=%async_computation | async-start | bytes 1048576 | tf_op jit(solution)/shard_map/all_to_all | solution.py:28
  13.8 94.3 %all-gather.3.cloned.1.call-start = ((), (), s32[]{:S(2)}) async-start(), calls=%async_computation.7 | async-start | bytes 4325376 | tf_op jit(solution)/shard_map/all_gather | solution.py:56
  14.9 2.2 copy-start.9
  126.0 15.9 %copy-start.7 = (f32[512]{0:T(512)S(1)}, f32[512]{0:T(512)}, u32[]{:S(2)}) copy-start(f32[512]{0:T(512)} %param.17) | copy-start | bytes 6148
  126.9 16.2 %copy-start.2 = (bf16[256,512]{1,0:T(8,128)(2,1)S(1)}, bf16[256,512]{1,0:T(8,128)(2,1)}, u32[]{:S(2)}) copy-start(bf16[256,512]{1,0:T(8,128)(2,1)} %param.18) | copy-start | bytes 786436
  126.9 14.8 %all-to-all-start.1 = ((bf16[8,256,128]{2,1,0:T(8,128)(2,1)}), bf16[8,256,128]{2,1,0:T(8,128)(2,1)S(1)}, u32[]{:S(2)}, u32[]{:S(2)}) async-start(bf16[8,256,128]{2,1,0:T(8,128)(2,1)} %bitcast.15), calls=%async_computation.1 | async-start | bytes 1048576 | tf_op jit(solution)/shard_map/all_to_all | solution.py:68
  144.6 13.8 %all-to-all-start.2 = ((bf16[256,8,128]{2,0,1:T(8,128)(2,1)}), bf16[256,8,128]{2,0,1:T(8,128)(2,1)S(1)}, u32[]{:S(2)}, u32[]{:S(2)}) async-start(bf16[256,8,128]{2,0,1:T(8,128)(2,1)} %bitcast.76), calls=%async_computation.2 | async-start | bytes 1048576 | tf_op jit(solution)/shard_map/all_to_all | solution.py:79
  148.1 260.6 %reduce-scatter.2.cloned.1.call-start = ((), (), s32[]{:S(2)}) async-start(), calls=%async_computation.5 | async-start | bytes 8650752 | tf_op jit(solution)/shard_map/reduce_scatter | solution.py:104
  183.5 492.5 %all-reduce.2.cloned.1.call-start = ((), (), s32[]{:S(2)}) async-start(), calls=%async_computation.6 | async-start | bytes 4194304 | tf_op jit(solution)/shard_map/psum | solution.py:115
  413.3 265.9 %all-to-all-start.3 = ((bf16[8,256,128]{2,1,0:T(8,128)(2,1)}), bf16[8,256,128]{2,1,0:T(8,128)(2,1)S(1)}, u32[]{:S(2)}, u32[]{:S(2)}) async-start(bf16[8,256,128]{2,1,0:T(8,128)(2,1)} %bitcast.26), calls=%async_computation.4 | async-start | bytes 1048576 | tf_op jit(solution)/shard_map/all_to_all | solution.py:107
Sparse Core Ops, SparseCore 0:
  26.6 81.3 all-gather.2
  183.6 225.0 reduce-scatter.1
  415.5 260.4 all-reduce.1
where the time goes:
time: 691 us; the launch traced here: 687 us
  waiting for transfers between devices  341 us (49%)
  local copies, waits for them, and re-layouts  94.3 us (14%)
  other arithmetic  85.3 us (12%)
  blocking collectives  75.8 us (11%)
  matrix products  58.9 us (9%)
  starting transfers between devices  16.8 us (2%)
  between operations  14 us (2%)
    psum x1, waiting for transfers between devices, per_device(): lax.psum((weight_part, bias_part), ('dom', 'grp'))  258 us
    psum x1, blocking collectives, per_device(): lax.psum((weight_part, bias_part), ('dom', 'grp'))  75.8 us
    scatter-add x16, other arithmetic, backward_tiles(): return running + jax.ops.segment_sum(contrib, column, num_segments=blocks)  53.1 us
    reduce_scatter x1, waiting for transfers between devices, per_device(): mine_back = lax.psum_scatter(placed, 'dom', scatter_dimension=0, tiled=True)  48.2 us
    gather x16, local copies, waits for them, and re-layouts, forward_tiles(): feat_blocks[column]  39.2 us
    dot_general x16, matrix products, forward_tiles(): jnp.einsum('rij,rjf->rif', tile_bank[bank_ids], feat_blocks[column], pref...  23.2 us
    gather x16, local copies, waits for them, and re-layouts, backward_tiles(): tile_bank[bank_ids]  22.5 us
    dot_general x16, matrix products, backward_tiles(): jnp.einsum('rji,rjf->rif', tile_bank[bank_ids], grad_blocks, preferred_el...  22.3 us
  transfers between devices with their start and end apart: 7, of which 6 were waited for; matrix products, arithmetic and copies ran while one was open for 27% of the time, Pallas kernels for 0%

commit v1 on v0

--- a/solution.py
+++ b/solution.py
@@ -2,6 +2,8 @@
 import jax.numpy as jnp
 from jax import lax
 from jax.sharding import PartitionSpec as P
+
+limits_move = lambda view: lax.psum(lax.psum(view, "grp"), "dom")
 
 
 def per_device(
@@ -112,7 +114,7 @@
         tiled=True,
     )
     norm_scale = float(rows_here * groups * domains) ** (-0.5)
-    weight_total, bias_total = lax.psum((weight_part, bias_part), ("dom", "grp"))
+    weight_total, bias_total = limits_move((weight_part, bias_part))
     return (activations, grad_nodes, weight_total * norm_scale, bias_total * norm_scale)
 
 

time: 691 us -> 619 us (0.90)
  waiting for transfers between devices: 341 us -> 266 us
    psum x1 -> x2, waiting for transfers between devices: 258 us -> 146 us  [limits_move = lambda view: lax.psum(lax.psum(view, 'grp'), 'dom')]
    reduce_scatter x1, waiting for transfers between devices: 48.2 us -> 82.5 us  [per_device(): mine_back = lax.psum_scatter(placed, 'dom', scatter_dimension=0, tiled=True)]
    psum x1 -> x2, blocking collectives: 75.8 us -> 76.6 us  [limits_move = lambda view: lax.psum(lax.psum(view, 'grp'), 'dom')]
  transfers between devices with their start and end apart: 7 -> 8, of which waited for: 6 -> 6; matrix products, arithmetic and copies ran while one was open for 27% -> 34% of each run, Pallas kernels for 0% -> 0%
where the time goes in v1:
time: 619 us; the launch traced here: 613 us
  waiting for transfers between devices  266 us (43%)
  local copies, waits for them, and re-layouts  94.3 us (15%)
  other arithmetic  85 us (14%)
  blocking collectives  76.6 us (12%)
  matrix products  59 us (10%)
  starting transfers between devices  16.8 us (3%)
  between operations  14.1 us (2%)
    psum x2, waiting for transfers between devices, limits_move = lambda view: lax.psum(lax.psum(view, 'grp'), 'dom')  146 us
    reduce_scatter x1, waiting for transfers between devices, per_device(): mine_back = lax.psum_scatter(placed, 'dom', scatter_dimension=0, tiled=True)  82.5 us
    psum x2, blocking collectives, limits_move = lambda view: lax.psum(lax.psum(view, 'grp'), 'dom')  76.6 us
    scatter-add x16, other arithmetic, backward_tiles(): return running + jax.ops.segment_sum(contrib, column, num_segments=blocks)  52.7 us
    gather x16, local copies, waits for them, and re-layouts, forward_tiles(): feat_blocks[column]  39.2 us
    dot_general x16, matrix products, forward_tiles(): jnp.einsum('rij,rjf->rif', tile_bank[bank_ids], feat_blocks[column], pref...  23.2 us
    gather x16, local copies, waits for them, and re-layouts, backward_tiles(): tile_bank[bank_ids]  22.5 us
    dot_general x16, matrix products, backward_tiles(): jnp.einsum('rji,rjf->rif', tile_bank[bank_ids], grad_blocks, preferred_el...  22.3 us
  transfers between devices with their start and end apart: 8, of which 6 were waited for; matrix products, arithmetic and copies ran while one was open for 34% of the time, Pallas kernels for 0%

profile of v1, /device:TPU:2, one launch (start us, length us, event | category | flops | bytes accessed | tf_op | source)
XLA Modules:
  0.0 612.8 jit_solution(13723840130877522859)
XLA Ops:
  9.3 4.5 all-to-all-start
  17.1 7.1 %all-to-all-done = bf16[256,8,128]{2,0,1:T(8,128)(2,1)} async-done(((bf16[256,8,128]{2,0,1:T(8,128)(2,1)}), bf16[256,8,128]{2,0,1:T(8,128)(2,1)}, u32[]{:S(2)}, u32[]{:S(2)}) %all-to-all-start) | async-done | bytes 524320 | tf_op jit(solution)/shard_map/all_to_all | solution.py:30
  26.5 74.0 %while.28 = (s32[]{:T(128)}, f32[16,128,128]{2,1,0:T(8,128)S(1)}, s32[16,16]{0,1:T(8,128)S(1)}, bf16[16,128,128]{2,1,0:T(8,128)(2,1)S(1)}, s32[16,16]{0,1:T(8,12...) while((s32[]{:T(128)}, f32[16,128,128]{2,1,0:T(8,128)S(1)}, ...), condition=%wide.region_1.2_spmd.clone, body=%wide.region_0.1_spmd.clone.sunk | while | flops 67635296 | bytes 5251683 | solution.py:54
  100.5 7.6 %all-gather.3.cloned.1.call-done = bf16[128,128,128]{2,1,0:T(8,128)(2,1)} async-done(((bf16[4,128,128]{2,1,0:T(8,128)(2,1)}), bf16[128,128,128]{2,1,0:T(8,128)(2,1)}) %all-gather.3.cloned.1.call-update) | async-done | bytes 4194320 | tf_op jit(solution)/shard_map/all_gather | solution.py:58
  108.1 4.3 gather_fusion.5
  112.4 4.9 convolution_multiply_fusion.1
  117.2 8.8 %scatter_fusion.1 = f32[16,128,128]{2,1,0:T(8,128)S(1)} fusion(f32[16,128,128]{2,1,0:T(8,128)S(1)} %get-tuple-element.222, s32[64]{0:T(128)S(1)} %reshape.272, f32[64,128,128]{2,1,0:T(8,128)} %bitcast.94), kind=kCustom, calls=%fused_computation.8 | custom fusion | flops 1048576 | bytes 12583168 | tf_op jit(solution)/shard_map/scatter-add | solution.py:64
  126.9 4.4 all-to-all-start.1
  131.6 10.1 %all-to-all-done.1 = bf16[8,256,128]{2,1,0:T(8,128)(2,1)S(1)} async-done(((bf16[8,256,128]{2,1,0:T(8,128)(2,1)}), bf16[8,256,128]{2,1,0:T(8,128)(2,1)S(1)}, u32[]{:S(2)}, u32[]{:S(2)}) %all-to-all-start.1) | async-done | bytes 524320 | tf_op jit(solution)/shard_map/all_to_all | solution.py:70
  146.4 3.5 all-to-all-start.2
  150.3 12.3 %all-to-all-done.2 = bf16[256,8,128]{2,0,1:T(8,128)(2,1)S(1)} async-done(((bf16[256,8,128]{2,0,1:T(8,128)(2,1)}), bf16[256,8,128]{2,0,1:T(8,128)(2,1)S(1)}, u32[]{:S(2)}, u32[]{:S(2)}) %all-to-all-start.2) | async-done | bytes 524320 | tf_op jit(solution)/shard_map/all_to_all | solution.py:81
  164.8 5.3 convolution_multiply_fusion
  170.1 4.3 broadcast_in_dim.12
  174.3 13.5 %scatter_fusion.2 = f32[128,128,128]{2,1,0:T(8,128)} fusion(f32[128,128,128]{2,1,0:T(8,128)} %broadcast_in_dim.12, s32[64]{0:T(128)S(1)} %add_bitcast_fusion, f32[64,128,128]{2,1,0:T(8,128)} %bitcast.93), kind=kCustom, calls=%fused_computation.9 | custom fusion | flops 1048576 | bytes 12583168 | tf_op jit(solution)/shard_map/scatter-add | solution.py:101
  187.9 12.5 %psum.30 = f32[512]{0:T(512)S(1)} all-reduce(f32[512]{0:T(512)S(1)} %get-tuple-element.277), channel_id=1, replica_groups=mesh['dom'=32,'grp'=8] {'grp'}, use_global_device_ids=true, to_apply=%region_12.13 | all-reduce | flops 512 | bytes 4096 | tf_op jit(solution)/shard_map/psum | solution.py:6
  200.4 64.2 %psum.31 = f32[512]{0:T(512)S(1)} all-reduce(f32[512]{0:T(512)S(1)} %psum.30), channel_id=1, replica_groups=mesh['dom'=32,'grp'=8] {'dom'}, use_global_device_ids=true, to_apply=%region_13.14 | all-reduce | flops 512 | bytes 4096 | tf_op jit(solution)/shard_map/psum | solution.py:6
  265.7 97.9 %while.27 = (s32[]{:T(128)}, f32[16,128,128]{2,1,0:T(8,128)}, s32[16,16]{0,1:T(8,128)S(1)}, s32[16,16]{0,1:T(8,128)S(1)}, bf16[16,128,128]{2,1,0:T(8,128)(2,1)S(...) while((s32[]{:T(128)}, f32[16,128,128]{2,1,0:T(8,128)}, s32[16,16]{0,1:T(8,128)S(1)}, ...), condition=%wide.region_5.6_spmd, body=%wide.region_3.5_spmd.sunk | while | flops 67372080 | bytes 6296081 | solution.py:92
  268.5 3.3 scatter_fusion
  293.0 3.3 scatter_fusion
  311.4 3.3 scatter_fusion
  323.6 3.3 scatter_fusion
  363.6 82.5 %reduce-scatter.2.cloned.1.call-done = f32[4,128,128]{2,1,0:T(8,128)} async-done(((f32[128,128,128]{2,1,0:T(8,128)}), f32[4,128,128]{2,1,0:T(8,128)}) %reduce-scatter.2.cloned.1.call-update) | async-done | bytes 262160 | tf_op jit(solution)/shard_map/reduce_scatter | solution.py:106
  450.7 4.3 all-to-all-start.3
  455.6 146.3 %all-reduce.5.cloned.1.call-done = f32[1024,512]{1,0:T(8,128)} async-done(((f32[1024,512]{1,0:T(8,128)}), f32[1024,512]{1,0:T(8,128)}) %all-reduce.5.cloned.1.call-update) | async-done | bytes 2097168 | tf_op jit(solution)/shard_map/psum | solution.py:6
  (250 shorter events, 184.1 us)
Async XLA Ops:
  7.2 134.8 %copy-start = (bf16[1024,512]{1,0:T(8,128)(2,1)S(1)}, bf16[1024,512]{1,0:T(8,128)(2,1)}, u32[]{:S(2)}) copy-start(bf16[1024,512]{1,0:T(8,128)(2,1)} %param.16) | copy-start | bytes 3145732
  7.2 6.6 %copy-start.3 = (s32[32,32,2]{1,2,0:T(2,128)S(1)}, s32[32,32,2]{1,2,0:T(2,128)}, u32[]{:S(2)}) copy-start(s32[32,32,2]{1,2,0:T(2,128)} %param.23) | copy-start | bytes 24580
  7.2 6.8 %copy-start.8 = (s32[1,32,2]{1,2,0:T(2,128)S(1)}, s32[1,32,2]{1,2,0:T(2,128)}, u32[]{:S(2)}) copy-start(s32[1,32,2]{1,2,0:T(2,128)} %param.25) | copy-start | bytes 772
  7.2 7.4 %copy-start.4 = (s32[1,16,16]{2,1,0:T(8,128)S(1)}, s32[1,16,16]{2,1,0:T(8,128)}, u32[]{:S(2)}) copy-start(s32[1,16,16]{2,1,0:T(8,128)} %param.21) | copy-start | bytes 3076
  7.2 7.4 %copy-start.5 = (s32[1,16,16]{2,1,0:T(8,128)S(1)}, s32[1,16,16]{2,1,0:T(8,128)}, u32[]{:S(2)}) copy-start(s32[1,16,16]{2,1,0:T(8,128)} %param.20) | copy-start | bytes 3076
  7.2 7.5 %copy-start.6 = (s32[1,32,2]{1,2,0:T(2,128)S(1)}, s32[1,32,2]{1,2,0:T(2,128)}, u32[]{:S(2)}) copy-start(s32[1,32,2]{1,2,0:T(2,128)} %param.24) | copy-start | bytes 772
  7.2 7.7 %copy-start.1 = (bf16[16,128,128]{2,1,0:T(8,128)(2,1)S(1)}, bf16[16,128,128]{2,1,0:T(8,128)(2,1)}, u32[]{:S(2)}) copy-start(bf16[16,128,128]{2,1,0:T(8,128)(2,1)} %param.19) | copy-start | bytes 1572868
  9.3 14.9 %all-to-all-start = ((bf16[256,8,128]{2,0,1:T(8,128)(2,1)}), bf16[256,8,128]{2,0,1:T(8,128)(2,1)}, u32[]{:S(2)}, u32[]{:S(2)}) async-start(bf16[256,8,128]{2,0,1:T(8,128)(2,1)} %copy_bitcast_fusion.1), calls=%async_computation | async-start | bytes 1048576 | tf_op jit(solution)/shard_map/all_to_all | solution.py:30
  13.8 94.3 %all-gather.3.cloned.1.call-start = ((), (), s32[]{:S(2)}) async-start(), calls=%async_computation.8 | async-start | bytes 4325376 | tf_op jit(solution)/shard_map/all_gather | solution.py:58
  14.9 2.2 copy-start.9
  126.0 15.9 %copy-start.7 = (f32[512]{0:T(512)S(1)}, f32[512]{0:T(512)}, u32[]{:S(2)}) copy-start(f32[512]{0:T(512)} %param.17) | copy-start | bytes 6148
  126.9 16.2 %copy-start.2 = (bf16[256,512]{1,0:T(8,128)(2,1)S(1)}, bf16[256,512]{1,0:T(8,128)(2,1)}, u32[]{:S(2)}) copy-start(bf16[256,512]{1,0:T(8,128)(2,1)} %param.18) | copy-start | bytes 786436
  126.9 14.8 %all-to-all-start.1 = ((bf16[8,256,128]{2,1,0:T(8,128)(2,1)}), bf16[8,256,128]{2,1,0:T(8,128)(2,1)S(1)}, u32[]{:S(2)}, u32[]{:S(2)}) async-start(bf16[8,256,128]{2,1,0:T(8,128)(2,1)} %bitcast.15), calls=%async_computation.1 | async-start | bytes 1048576 | tf_op jit(solution)/shard_map/all_to_all | solution.py:70
  131.4 133.2 %all-reduce.3.cloned.1.call-start = ((), (), s32[]{:S(2)}) async-start(), calls=%async_computation.6 | async-start | bytes 4194304 | tf_op jit(solution)/shard_map/psum | solution.py:6
  146.4 16.2 %all-to-all-start.2 = ((bf16[256,8,128]{2,0,1:T(8,128)(2,1)}), bf16[256,8,128]{2,0,1:T(8,128)(2,1)S(1)}, u32[]{:S(2)}, u32[]{:S(2)}) async-start(bf16[256,8,128]{2,0,1:T(8,128)(2,1)} %bitcast.76), calls=%async_computation.2 | async-start | bytes 1048576 | tf_op jit(solution)/shard_map/all_to_all | solution.py:81
  149.9 296.2 %reduce-scatter.2.cloned.1.call-start = ((), (), s32[]{:S(2)}) async-start(), calls=%async_computation.5 | async-start | bytes 8650752 | tf_op jit(solution)/shard_map/reduce_scatter | solution.py:106
  187.9 414.0 %all-reduce.5.cloned.1.call-start = ((), (), s32[]{:S(2)}) async-start(), calls=%async_computation.7 | async-start | bytes 4194304 | tf_op jit(solution)/shard_map/psum | solution.py:6
  450.7 154.4 %all-to-all-start.3 = ((bf16[8,256,128]{2,1,0:T(8,128)(2,1)}), bf16[8,256,128]{2,1,0:T(8,128)(2,1)S(1)}, u32[]{:S(2)}, u32[]{:S(2)}) async-start(bf16[8,256,128]{2,1,0:T(8,128)(2,1)} %bitcast.26), calls=%async_computation.4 | async-start | bytes 1048576 | tf_op jit(solution)/shard_map/all_to_all | solution.py:109
Sparse Core Ops, SparseCore 0:
  26.6 81.3 all-gather.2
  145.1 69.2 all-reduce.2
  218.5 227.5 reduce-scatter.1
  449.9 151.9 all-reduce.4
